TPU v7x, 32 devices: a whole 2x2x4 slice. The times are simulated.
32 devices in a mesh: dp: 8 (over z, core), mp: 4 (over y, x).
Axes of the slice: x: 2, y: 2, z: 4, core: 2. Of those that a mesh axis runs over, the one named last changes fastest.
Arguments:
- tokens: bfloat16 [12288, 2048], P(('dp', 'mp')), may hold values from -6 to 6
- segment_ids: int32 [16, 768], P('dp'), may hold values from 0 to 5, never falling along the last dimension, each value on 1 to 256 neighbouring positions
- query_weight: bfloat16 [2048, 2048], P(None, 'mp'), may hold values from -0.125 to 0.125
- key_weight: bfloat16 [2048, 2048], P(None, 'mp'), may hold values from -0.125 to 0.125
- value_weight: bfloat16 [2048, 2048], P(None, 'mp'), may hold values from -0.125 to 0.125
- out_weight: bfloat16 [2048, 2048], P('mp'), may hold values from -0.75 to 0.75
- up_weight: bfloat16 [2048, 8192], P(None, 'mp'), may hold values from -0.125 to 0.125
- down_weight: bfloat16 [8192, 2048], P('mp'), may hold values from -0.0625 to 0.0625
- attn_gain: float32 [2048], replicated, may hold values from 0.5 to 1.5
- mlp_gain: float32 [2048], replicated, may hold values from 0.5 to 1.5
- out_cotangent: bfloat16 [12288, 2048], P(('dp', 'mp')), may hold values from -18 to 18
Outputs:
- layer_output: bfloat16 [12288, 2048], P(('dp', 'mp'))
- tokens_grad: float32 [12288, 2048], P(('dp', 'mp'))
- query_weight_grad: float32 [2048, 2048], P('dp', 'mp')
- key_weight_grad: float32 [2048, 2048], P('dp', 'mp')
- value_weight_grad: float32 [2048, 2048], P('dp', 'mp')
- out_weight_grad: float32 [2048, 2048], P('mp', 'dp')
- up_weight_grad: float32 [2048, 8192], P('dp', 'mp')
- down_weight_grad: float32 [8192, 2048], P('mp', 'dp')
- attn_gain_grad: float32 [2048], replicated
- mlp_gain_grad: float32 [2048], replicated
Inputs may be any that keep to these rules, and one draw needn't show every extreme that they name: `segment_ids`: within each packed sequence the clip numbers never fall; each clip covers 1 to 256 tokens, and some clip covers exactly 256.
All inputs are finite; a program needn't handle non-finite values.
Results may differ from a plain program's by a relative error of at most 0.02.
Values may be sent and summed in bfloat16 or wider, within the bound.
A program may use at most 192 MiB of HBM per device.

v0:
```python
import math
import jax
import jax.numpy as jnp
from jax import lax
from jax.sharding import PartitionSpec as P

HEAD_DIM = 128
epsilon = 1e-05
masked_score = -1e30


def norm_rows(values, gain):
    centre = jnp.mean(values, axis=-1, keepdims=True)
    centred = values - centre
    spread = jnp.mean(centred * centred, axis=-1, keepdims=True)
    return centred * lax.rsqrt(spread + epsilon) * gain


def gelu_tanh(values):
    return jax.nn.gelu(values, approximate=True)


def block_allowed(segment):
    position = jnp.arange(segment.shape[0])
    return (position[None, :] <= position[:, None]) & (segment[:, None] == segment[None, :])


def rows_times(left_rows, right_matrix):
    return jnp.dot(left_rows, right_matrix, preferred_element_type=jnp.float32)


def rows_times_back(left_rows, right_matrix):
    return lax.dot_general(
        left_rows, right_matrix, (((1,), (1,)), ((), ())), preferred_element_type=jnp.float32
    )


def attn_input_back(
    queries_grad, keys_grad, values_grad, query_weight, key_weight, value_weight, score_scale
):
    total_grad = rows_times_back(queries_grad, query_weight) * score_scale
    total_grad = total_grad + rows_times_back(keys_grad, key_weight)
    return total_grad + rows_times_back(values_grad, value_weight)


def attend_forward(packed):
    queries, keys_in, values_in, segment = packed
    scores = jnp.einsum("qhd,khd->hqk", queries, keys_in, preferred_element_type=jnp.float32)
    scores = jnp.where(block_allowed(segment)[None], scores, masked_score)
    row_max = jnp.max(scores, axis=-1, keepdims=True)
    expanded = jnp.exp(scores - row_max)
    row_total = jnp.sum(expanded, axis=-1, keepdims=True)
    probs_low = (expanded / row_total).astype(jnp.bfloat16)
    context = jnp.einsum("hqk,khd->qhd", probs_low, values_in, preferred_element_type=jnp.float32)
    return (context.astype(jnp.bfloat16), (row_max + jnp.log(row_total))[:, :, 0])


def attend_backward(packed):
    queries, keys_in, values_in, segment, context_grad, log_total = packed
    scores = jnp.einsum("qhd,khd->hqk", queries, keys_in, preferred_element_type=jnp.float32)
    scores = jnp.where(block_allowed(segment)[None], scores, masked_score)
    attn_probs = jnp.exp(scores - log_total[:, :, None])
    probs_grad = jnp.einsum(
        "qhd,khd->hqk", context_grad, values_in, preferred_element_type=jnp.float32
    )
    values_grad = jnp.einsum(
        "hqk,qhd->khd",
        attn_probs.astype(jnp.bfloat16),
        context_grad,
        preferred_element_type=jnp.float32,
    )
    inner_sum = jnp.sum(attn_probs * probs_grad, axis=-1, keepdims=True)
    scores_grad = (attn_probs * (probs_grad - inner_sum)).astype(jnp.bfloat16)
    queries_grad = jnp.einsum(
        "hqk,khd->qhd", scores_grad, keys_in, preferred_element_type=jnp.float32
    )
    keys_grad = jnp.einsum("hqk,qhd->khd", scores_grad, queries, preferred_element_type=jnp.float32)
    return (
        queries_grad.astype(jnp.bfloat16),
        keys_grad.astype(jnp.bfloat16),
        values_grad.astype(jnp.bfloat16),
    )


def local(
    tokens,
    segment_ids,
    query_weight,
    key_weight,
    value_weight,
    out_weight,
    up_weight,
    down_weight,
    attn_gain,
    mlp_gain,
    out_cotangent,
):
    seq_count, seq_length = segment_ids.shape
    group_rows = seq_count * seq_length
    head_count = query_weight.shape[1] // HEAD_DIM
    score_scale = 1.0 / math.sqrt(HEAD_DIM)
    shaped = (seq_count, seq_length, head_count, HEAD_DIM)
    flat_shape = (group_rows, head_count * HEAD_DIM)
    residual_in = tokens.astype(jnp.float32)
    normed_attn, attn_norm_back = jax.vjp(norm_rows, residual_in, attn_gain)
    gathered_attn = lax.all_gather(normed_attn.astype(jnp.bfloat16), "mp", axis=0, tiled=True)
    queries = (
        jnp.dot(gathered_attn, query_weight, preferred_element_type=jnp.float32) * score_scale
    ).astype(jnp.bfloat16)
    keys_all = jnp.dot(gathered_attn, key_weight, preferred_element_type=jnp.float32).astype(
        jnp.bfloat16
    )
    values_all = jnp.dot(gathered_attn, value_weight, preferred_element_type=jnp.float32).astype(
        jnp.bfloat16
    )
    queries_seq = queries.reshape(shaped)
    keys_seq = keys_all.reshape(shaped)
    values_seq = values_all.reshape(shaped)
    context, log_total = lax.map(attend_forward, (queries_seq, keys_seq, values_seq, segment_ids))
    context_flat = context.reshape(flat_shape)
    attn_rows = lax.psum_scatter(
        rows_times(context_flat, out_weight).astype(jnp.bfloat16),
        "mp",
        scatter_dimension=0,
        tiled=True,
    ).astype(jnp.float32)
    residual_mid = residual_in + attn_rows
    normed_mlp, mlp_norm_back = jax.vjp(norm_rows, residual_mid, mlp_gain)
    gathered_mlp = lax.all_gather(normed_mlp.astype(jnp.bfloat16), "mp", axis=0, tiled=True)
    pre_act = jnp.dot(gathered_mlp, up_weight, preferred_element_type=jnp.float32)
    activated, gelu_back = jax.vjp(gelu_tanh, pre_act)
    hidden = activated.astype(jnp.bfloat16)
    mlp_rows = lax.psum_scatter(
        rows_times(hidden, down_weight).astype(jnp.bfloat16), "mp", scatter_dimension=0, tiled=True
    ).astype(jnp.float32)
    layer_output = (residual_mid + mlp_rows).astype(jnp.bfloat16)
    cotangent_all = lax.all_gather(out_cotangent, "mp", axis=0, tiled=True)
    down_weight_grad = jnp.einsum(
        "rf,rd->fd", hidden, cotangent_all, preferred_element_type=jnp.float32
    )
    hidden_grad = lax.dot_general(
        cotangent_all, down_weight, (((1,), (1,)), ((), ())), preferred_element_type=jnp.float32
    )
    pre_grad = gelu_back(hidden_grad)[0].astype(jnp.bfloat16)
    up_weight_grad = jnp.einsum(
        "rd,rf->df", gathered_mlp, pre_grad, preferred_element_type=jnp.float32
    )
    normed_mlp_grad = lax.psum_scatter(
        rows_times_back(pre_grad, up_weight).astype(jnp.bfloat16),
        "mp",
        scatter_dimension=0,
        tiled=True,
    ).astype(jnp.float32)
    middle_back, mlp_gain_grad = mlp_norm_back(normed_mlp_grad)
    middle_grad = out_cotangent.astype(jnp.float32) + middle_back
    middle_all_grad = lax.all_gather(middle_grad.astype(jnp.bfloat16), "mp", axis=0, tiled=True)
    out_weight_grad = jnp.einsum(
        "rc,rd->cd", context_flat, middle_all_grad, preferred_element_type=jnp.float32
    )
    context_grad = lax.dot_general(
        middle_all_grad, out_weight, (((1,), (1,)), ((), ())), preferred_element_type=jnp.float32
    ).astype(jnp.bfloat16)
    queries_grad, keys_grad, values_grad = lax.map(
        attend_backward,
        (queries_seq, keys_seq, values_seq, segment_ids, context_grad.reshape(shaped), log_total),
    )
    queries_grad = queries_grad.reshape(flat_shape)
    keys_grad = keys_grad.reshape(flat_shape)
    values_grad = values_grad.reshape(flat_shape)
    query_weight_grad = (
        jnp.einsum("rd,rc->dc", gathered_attn, queries_grad, preferred_element_type=jnp.float32)
        * score_scale
    )
    key_weight_grad = jnp.einsum(
        "rd,rc->dc", gathered_attn, keys_grad, preferred_element_type=jnp.float32
    )
    value_weight_grad = jnp.einsum(
        "rd,rc->dc", gathered_attn, values_grad, preferred_element_type=jnp.float32
    )
    normed_attn_grad = lax.psum_scatter(
        attn_input_back(
            queries_grad,
            keys_grad,
            values_grad,
            query_weight,
            key_weight,
            value_weight,
            score_scale,
        ).astype(jnp.bfloat16),
        "mp",
        scatter_dimension=0,
        tiled=True,
    ).astype(jnp.float32)
    token_back, attn_gain_grad = attn_norm_back(normed_attn_grad)
    tokens_grad = middle_grad + token_back
    attn_gain_grad, mlp_gain_grad = lax.psum((attn_gain_grad, mlp_gain_grad), ("dp", "mp"))
    (
        query_weight_grad,
        key_weight_grad,
        value_weight_grad,
        out_weight_grad,
        up_weight_grad,
        down_weight_grad,
    ) = (
        lax.psum_scatter(
            query_weight_grad.astype(jnp.bfloat16), "dp", scatter_dimension=0, tiled=True
        ).astype(jnp.float32),
        lax.psum_scatter(
            key_weight_grad.astype(jnp.bfloat16), "dp", scatter_dimension=0, tiled=True
        ).astype(jnp.float32),
        lax.psum_scatter(
            value_weight_grad.astype(jnp.bfloat16), "dp", scatter_dimension=0, tiled=True
        ).astype(jnp.float32),
        lax.psum_scatter(
            out_weight_grad.astype(jnp.bfloat16), "dp", scatter_dimension=1, tiled=True
        ).astype(jnp.float32),
        lax.psum_scatter(
            up_weight_grad.astype(jnp.bfloat16), "dp", scatter_dimension=0, tiled=True
        ).astype(jnp.float32),
        lax.psum_scatter(
            down_weight_grad.astype(jnp.bfloat16), "dp", scatter_dimension=1, tiled=True
        ).astype(jnp.float32),
    )
    return (
        layer_output,
        tokens_grad,
        query_weight_grad,
        key_weight_grad,
        value_weight_grad,
        out_weight_grad,
        up_weight_grad,
        down_weight_grad,
        attn_gain_grad,
        mlp_gain_grad,
    )


def solution(mesh):
    return jax.shard_map(
        local,
        mesh=mesh,
        in_specs=(
            P(("dp", "mp"), None),
            P("dp", None),
            P(None, "mp"),
            P(None, "mp"),
            P(None, "mp"),
            P("mp", None),
            P(None, "mp"),
            P("mp", None),
            P(),
            P(),
            P(("dp", "mp"), None),
        ),
        out_specs=(
            P(("dp", "mp"), None),
            P(("dp", "mp"), None),
            P("dp", "mp"),
            P("dp", "mp"),
            P("dp", "mp"),
            P("mp", "dp"),
            P("dp", "mp"),
            P("mp", "dp"),
            P(),
            P(),
        ),
        check_vma=False,
    )
```

profile of v0, /device:TPU:0, one launch (start us, length us, event | category | flops | bytes accessed | tf_op | source)
XLA Modules:
  0.0 1105.6 jit_solution(7210589673843302547)
XLA Ops:
  14.0 73.0 %all-gather.5.cloned.1.call-done = bf16[1536,2048]{1,0:T(8,128)(2,1)} async-done(((bf16[384,2048]{1,0:T(8,128)(2,1)}), bf16[1536,2048]{1,0:T(8,128)(2,1)}) %all-gather.5.cloned.1.call-update) | async-done | bytes 6291472 | tf_op jit(solution)/shard_map/all_gather | solution.py:106
  127.6 28.2 %while.26 = (s32[]{:T(128)}, bf16[2,768,4,128]{3,2,1,0:T(4,128)(2,1)}, f32[2,4,768]{2,1,0:T(4,128)S(1)}, bf16[2,768,4,128]{3,2,1,0:T(4,128)(2,1)}, s32[2,768]{1,...) while((s32[]{:T(128)}, ...), condition=%wide.region_5.6_spmd, body=%wide.region_2.5_spmd.sunk | while | flops 1231352832 | bytes 43362440 | solution.py:119
  163.8 69.6 %reduce-scatter.11.cloned.1.call-done = bf16[384,2048]{1,0:T(8,128)(2,1)} async-done(((bf16[1536,2048]{1,0:T(8,128)(2,1)}), bf16[384,2048]{1,0:T(8,128)(2,1)}) %reduce-scatter.11.cloned.1.call-update) | async-done | bytes 1572880 | tf_op jit(solution)/shard_map/reduce_scatter | solution.py:121
  238.9 66.6 %all-gather.9.cloned.1.call-done = bf16[1536,2048]{1,0:T(8,128)(2,1)} async-done(((bf16[384,2048]{1,0:T(8,128)(2,1)}), bf16[1536,2048]{1,0:T(8,128)(2,1)}) %all-gather.9.cloned.1.call-update) | async-done | bytes 6291472 | tf_op jit(solution)/shard_map/all_gather | solution.py:137
  305.5 19.1 %fusion.89 = f32[1536,2048]{1,0:T(8,128)} fusion(bf16[1536,2048]{1,0:T(8,128)(2,1)} %all-gather.9.cloned.1.call-done, bf16[2048,2048]{1,0:T(8,128)(2,1)} %param.22), kind=kOutput, calls=%fused_computation.146 | convolution fusion | flops 12884901888 | bytes 27262976 | tf_op jit(solution)/shard_map/dot_general | solution.py:141
  324.5 53.4 %all-gather.7.cloned.1.call-done = bf16[1536,2048]{1,0:T(8,128)(2,1)} async-done(((bf16[384,2048]{1,0:T(8,128)(2,1)}), bf16[1536,2048]{1,0:T(8,128)(2,1)}) %all-gather.7.cloned.1.call-update) | async-done | bytes 6291472 | tf_op jit(solution)/shard_map/all_gather | solution.py:129
  377.9 29.6 %fusion.48 = (bf16[1536,2048]{1,0:T(8,128)(2,1)}, f32[1536,2048]{1,0:T(8,128)}) fusion(f32[1536,2048]{1,0:T(8,128)} %fusion.89, bf16[1536,2048]{1,0:T(8,128)(2,1)} %all-gather.7.cloned.1.call-done, bf16[2048,2048]{1,0:T(8,128)(2,1)} %param.21), kind=kOutput, calls=%fused_computation.68 | convolution fusion | flops 12947816448 | bytes 46137344 | tf_op jit(solution)/shard_map/dot_general | solution.py:130
  407.5 19.1 %convolution_convert_fusion.4 = bf16[1536,2048]{1,0:T(8,128)(2,1)} fusion(bf16[1536,2048]{1,0:T(8,128)(2,1)} %get-tuple-element.190, bf16[2048,2048]{1,0:T(8,128)(2,1)} %param.21), kind=kOutput, calls=%fused_computation.73 | convolution fusion | flops 12888047616 | bytes 20971520 | tf_op jit(solution)/shard_map/dot_general | solution.py:33
  426.7 20.5 %convolution_convert_fusion.5 = bf16[1536,2048]{1,0:T(8,128)(2,1)} fusion(bf16[2048,2048]{1,0:T(8,128)(2,1)} %param.22, f32[1536,2048]{1,0:T(8,128)} %get-tuple-element.191), kind=kOutput, calls=%fused_computation.74 | convolution fusion | flops 12916359168 | bytes 27262976 | tf_op jit(solution)/shard_map/dot_general | solution.py:29
  447.3 49.7 %reduce-scatter.15.cloned.1.call-done = bf16[384,2048]{1,0:T(8,128)(2,1)} async-done(((bf16[1536,2048]{1,0:T(8,128)(2,1)}), bf16[384,2048]{1,0:T(8,128)(2,1)}) %reduce-scatter.15.cloned.1.call-update) | async-done | bytes 1572880 | tf_op jit(solution)/shard_map/reduce_scatter | solution.py:148
  501.4 68.7 %reduce-scatter.13.cloned.1.call-done = bf16[384,2048]{1,0:T(8,128)(2,1)} async-done(((bf16[1536,2048]{1,0:T(8,128)(2,1)}), bf16[384,2048]{1,0:T(8,128)(2,1)}) %reduce-scatter.13.cloned.1.call-update) | async-done | bytes 1572880 | tf_op jit(solution)/shard_map/reduce_scatter | solution.py:133
  578.9 19.6 %convolution_convert_fusion.3 = bf16[2048,2048]{1,0:T(8,128)(2,1)} fusion(bf16[1536,2048]{1,0:T(8,128)(2,1)} %all-gather.7.cloned.1.call-done, bf16[1536,2048]{1,0:T(8,128)(2,1)} %get-tuple-element.190), kind=kOutput, calls=%fused_computation.72 | convolution fusion | flops 12889096192 | bytes 20971520 | tf_op jit(solution)/shard_map/rd,rf->df/dot_general | solution.py:145
  598.5 22.5 %convolution_convert_fusion.2 = bf16[2048,2048]{1,0:T(8,128)(2,1)} fusion(bf16[1536,2048]{1,0:T(8,128)(2,1)} %all-gather.9.cloned.1.call-done, f32[1536,2048]{1,0:T(8,128)} %get-tuple-element.191), kind=kOutput, calls=%fused_computation.71 | convolution fusion | flops 12917407744 | bytes 27262976 | tf_op jit(solution)/shard_map/rf,rd->fd/dot_general | solution.py:138
  621.1 28.0 %all-gather.11.cloned.1.call-done = bf16[1536,2048]{1,0:T(8,128)(2,1)} async-done(((bf16[384,2048]{1,0:T(8,128)(2,1)}), bf16[1536,2048]{1,0:T(8,128)(2,1)}) %all-gather.11.cloned.1.call-update) | async-done | bytes 6291472 | tf_op jit(solution)/shard_map/all_gather | solution.py:156
  673.6 99.9 %while.27 = (s32[]{:T(128)}, bf16[2,768,4,128]{3,2,1,0:T(4,128)(2,1)}, bf16[2,768,4,128]{3,2,1,0:T(4,128)(2,1)}, bf16[2,768,4,128]{3,2,1,0:T(4,128)(2,1)}, bf16[...) while((s32[]{:T(128)}, ...), condition=%wide.region_15.16_spmd, body=%wide.region_13.15_spmd.sunk | while | flops 3051156480 | bytes 169179440 | solution.py:163
  697.2 10.9 multiply_convert_fusion.7
  746.6 11.5 %multiply_convert_fusion.7 = bf16[4,768,768]{1,2,0:T(8,128)(2,1)} fusion(f32[4,768,768]{1,2,0:T(8,128)} %get-tuple-element.304, f32[4,768,768]{1,2,0:T(8,128)} %copy-done.1, f32[4,768]{1,0:T(4,128)S(1)} %get-tuple-element.305, f32[4,768]{1,0:T(4,128)S(1)} %dynamic-slice_bitcast_fusion.2, pred[768,768]{0,1:T(8,128)(4,1)S(1)} %fusion.146), kind=kLoop, calls=%fused_computation.21.clone.1 | loop fusion | flops 11796480 | bytes 24207360 | tf_op jit(solution)/shard_map/while/body/eval_jaxpr/convert_element_type | solution.py:73
  815.0 15.8 %add_convert_fusion = bf16[1536,2048]{1,0:T(8,128)(2,1)} fusion(f32[1536,2048]{1,0:T(8,128)} %fusion.69, f32[1536,2048]{1,0:T(8,128)} %fusion.72, bf16[2048,512]{1,0:T(8,128)(2,1)} %param.17, bf16[192,8,4,128]{3,2,1,0:T(4,128)(2,1)} %bitcast.147), kind=kOutput, calls=%fused_computation.69 | convolution fusion | flops 3233808384 | bytes 35127296 | tf_op jit(solution)/shard_map/dot_general | solution.py:33
  836.4 31.3 %reduce-scatter.25.cloned.1.call-done = bf16[512,256]{1,0:T(8,128)(2,1)} async-done(((bf16[512,2048]{1,0:T(8,128)(2,1)}), bf16[512,256]{1,0:T(8,128)(2,1)}) %reduce-scatter.25.cloned.1.call-update) | async-done | bytes 262160 | tf_op jit(solution)/shard_map/reduce_scatter | solution.py:214
  869.4 34.9 %reduce-scatter.19.cloned.1.call-done = bf16[256,512]{1,0:T(8,128)(2,1)} async-done(((bf16[2048,512]{1,0:T(8,128)(2,1)}), bf16[256,512]{1,0:T(8,128)(2,1)}) %reduce-scatter.19.cloned.1.call-update) | async-done | bytes 262160 | tf_op jit(solution)/shard_map/reduce_scatter | solution.py:205
  906.1 34.9 %reduce-scatter.23.cloned.1.call-done = bf16[256,512]{1,0:T(8,128)(2,1)} async-done(((bf16[2048,512]{1,0:T(8,128)(2,1)}), bf16[256,512]{1,0:T(8,128)(2,1)}) %reduce-scatter.23.cloned.1.call-update) | async-done | bytes 262160 | tf_op jit(solution)/shard_map/reduce_scatter | solution.py:211
  942.9 34.9 %reduce-scatter.21.cloned.1.call-done = bf16[256,512]{1,0:T(8,128)(2,1)} async-done(((bf16[2048,512]{1,0:T(8,128)(2,1)}), bf16[256,512]{1,0:T(8,128)(2,1)}) %reduce-scatter.21.cloned.1.call-update) | async-done | bytes 262160 | tf_op jit(solution)/shard_map/reduce_scatter | solution.py:208
  979.6 70.0 %reduce-scatter.17.cloned.1.call-done = bf16[384,2048]{1,0:T(8,128)(2,1)} async-done(((bf16[1536,2048]{1,0:T(8,128)(2,1)}), bf16[384,2048]{1,0:T(8,128)(2,1)}) %reduce-scatter.17.cloned.1.call-update) | async-done | bytes 1572880 | tf_op jit(solution)/shard_map/reduce_scatter | solution.py:180
  1054.0 39.5 %all-reduce = (f32[2048]{0:T(1024)}, f32[2048]{0:T(1024)}) all-reduce(f32[2048]{0:T(1024)S(1)} %get-tuple-element.143, f32[2048]{0:T(1024)S(1)} %copy-done.27), channel_id=1, replica_groups=mesh['dp'=8,'mp'=4] {'dp','mp'}, use_global_device_ids=true, to_apply=%region_26.27 | all-reduce | flops 4096 | bytes 32768 | tf_op jit(solution)/shard_map/psum | solution.py:196
  (208 shorter events, 267.6 us)
Async XLA Ops:
  7.2 148.6 %copy-start = (bf16[512,2048]{1,0:T(8,128)(2,1)S(1)}, bf16[512,2048]{1,0:T(8,128)(2,1)}, u32[]{:S(2)}) copy-start(bf16[512,2048]{1,0:T(8,128)(2,1)} %param.20) | copy-start | bytes 6291460
  7.2 79.8 %all-gather.5.cloned.1.call-start = ((), (), s32[]{:S(2)}) async-start(), calls=%async_computation.10 | async-start | bytes 7864320 | tf_op jit(solution)/shard_map/all_gather | solution.py:106
  13.9 219.5 %reduce-scatter.11.cloned.1.call-start = ((), (), s32[]{:S(2)}) async-start(), calls=%async_computation.11 | async-start | bytes 7864320 | tf_op jit(solution)/shard_map/reduce_scatter | solution.py:121
  163.1 142.4 %all-gather.9.cloned.1.call-start = ((), (), s32[]{:S(2)}) async-start(), calls=%async_computation.14 | async-start | bytes 7864320 | tf_op jit(solution)/shard_map/all_gather | solution.py:137
  163.1 73.9 %copy-start.24 = (f32[2048]{0:T(1024)S(1)}, f32[2048]{0:T(1024)}, u32[]{:S(2)}) copy-start(f32[2048]{0:T(1024)} %param.24) | copy-start | bytes 24580
  163.8 214.1 %all-gather.7.cloned.1.call-start = ((), (), s32[]{:S(2)}) async-start(), calls=%async_computation.12 | async-start | bytes 7864320 | tf_op jit(solution)/shard_map/all_gather | solution.py:129
  238.8 258.2 %reduce-scatter.15.cloned.1.call-start = ((), (), s32[]{:S(2)}) async-start(), calls=%async_computation.15 | async-start | bytes 7864320 | tf_op jit(solution)/shard_map/reduce_scatter | solution.py:148
  426.7 143.4 %reduce-scatter.13.cloned.1.call-start = ((), (), s32[]{:S(2)}) async-start(), calls=%async_computation.13 | async-start | bytes 7864320 | tf_op jit(solution)/shard_map/reduce_scatter | solution.py:133
  447.2 201.9 %all-gather.11.cloned.1.call-start = ((), (), s32[]{:S(2)}) async-start(), calls=%async_computation.16 | async-start | bytes 7864320 | tf_op jit(solution)/shard_map/all_gather | solution.py:156
  578.8 252.0 %reduce-scatter.27.cloned.1.call-start = ((), (), s32[]{:S(2)}) async-start(), calls=%async_computation.22 | async-start | bytes 9437184 | tf_op jit(solution)/shard_map/reduce_scatter | solution.py:217
  598.5 235.2 %reduce-scatter.29.cloned.1.call-start = ((), (), s32[]{:S(2)}) async-start(), calls=%async_computation.23 | async-start | bytes 9437184 | tf_op jit(solution)/shard_map/reduce_scatter | solution.py:220
  621.0 246.6 %reduce-scatter.25.cloned.1.call-start = ((), (), s32[]{:S(2)}) async-start(), calls=%async_computation.21 | async-start | bytes 2359296 | tf_op jit(solution)/shard_map/reduce_scatter | solution.py:214
  668.8 235.5 %reduce-scatter.19.cloned.1.call-start = ((), (), s32[]{:S(2)}) async-start(), calls=%async_computation.18 | async-start | bytes 2359296 | tf_op jit(solution)/shard_map/reduce_scatter | solution.py:205
  781.6 159.5 %reduce-scatter.23.cloned.1.call-start = ((), (), s32[]{:S(2)}) async-start(), calls=%async_computation.20 | async-start | bytes 2359296 | tf_op jit(solution)/shard_map/reduce_scatter | solution.py:211
  789.8 188.0 %reduce-scatter.21.cloned.1.call-start = ((), (), s32[]{:S(2)}) async-start(), calls=%async_computation.19 | async-start | bytes 2359296 | tf_op jit(solution)/shard_map/reduce_scatter | solution.py:208
  798.0 251.6 %reduce-scatter.17.cloned.1.call-start = ((), (), s32[]{:S(2)}) async-start(), calls=%async_computation.17 | async-start | bytes 7864320 | tf_op jit(solution)/shard_map/reduce_scatter | solution.py:180
  798.3 10.2 copy-start.15
  798.3 10.2 copy-start.33
  833.6 215.9 %copy-start.21 = (f32[2048]{0:T(1024)S(1)}, f32[2048]{0:T(1024)}, u32[]{:S(2)}) copy-start(f32[2048]{0:T(1024)} %param.23) | copy-start | bytes 24580
  833.6 215.9 %copy-start.23 = (f32[384]{0:T(512)S(1)}, f32[384]{0:T(512)}, u32[]{:S(2)}) copy-start(f32[384]{0:T(512)} %copy-done.22) | copy-start | bytes 4612
  836.4 216.0 %copy-start.31 = (f32[384]{0:T(512)S(1)}, f32[384]{0:T(512)}, u32[]{:S(2)}) copy-start(f32[384]{0:T(512)} %copy-done.30) | copy-start | bytes 4612
  836.4 216.0 %copy-start.26 = (f32[384]{0:T(512)S(1)}, f32[384]{0:T(512)}, u32[]{:S(2)}) copy-start(f32[384]{0:T(512)} %copy-done.25) | copy-start | bytes 4612
  979.6 74.4 %copy-start.27 = (f32[2048]{0:T(1024)S(1)}, f32[2048]{0:T(1024)}, u32[]{:S(2)}) copy-start(f32[2048]{0:T(1024)} %get-tuple-element.141) | copy-start | bytes 24580
  979.6 113.9 %copy-start.29 = (f32[384]{0:T(512)S(1)}, f32[384]{0:T(512)}, u32[]{:S(2)}) copy-start(f32[384]{0:T(512)} %copy-done.28) | copy-start | bytes 4612
  (30 other events, 109.6 us)
Sparse Core Ops, SparseCore 0:
  14.1 72.8 all-gather.4
  163.2 70.2 reduce-scatter.10
  235.3 70.1 all-gather.8
  307.7 70.1 all-gather.6
  426.8 70.1 reduce-scatter.14
  499.8 70.1 reduce-scatter.12
  579.0 70.1 all-gather.10
  651.4 89.5 reduce-scatter.26
  743.4 87.9 reduce-scatter.28
  833.5 34.0 reduce-scatter.24
  870.0 34.3 reduce-scatter.18
  906.5 34.5 reduce-scatter.22
  943.4 34.3 reduce-scatter.20
  980.6 68.8 reduce-scatter.16
where the time goes:
time: 1110 us
  waiting for transfers between devices  616 us (55%)
  matrix products  285 us (26%)
  local copies, waits for them, and re-layouts  78.1 us (7%)
  other arithmetic  71.6 us (6%)
  blocking collectives  39.5 us (4%)
  between operations  14.6 us (1%)
    all_gather x1, waiting for transfers between devices, local(): lax.all_gather(normed_attn.astype(jnp.bfloat16), 'mp', axis=0, tiled=True)  73 us
    reduce_scatter x1, waiting for transfers between devices, local(): lax.psum_scatter(attn_input_back(queries_grad, keys_grad, values_grad, qu...  70 us
    reduce_scatter x1, waiting for transfers between devices, local(): lax.psum_scatter(rows_times(context_flat, out_weight).astype(jnp.bfloat16...  69.6 us
    reduce_scatter x1, waiting for transfers between devices, local(): lax.psum_scatter(rows_times(hidden, down_weight).astype(jnp.bfloat16), 'm...  68.7 us
    all_gather x1, waiting for transfers between devices, local(): cotangent_all = lax.all_gather(out_cotangent, 'mp', axis=0, tiled=True)  66.6 us
    all_gather x1, waiting for transfers between devices, local(): lax.all_gather(normed_mlp.astype(jnp.bfloat16), 'mp', axis=0, tiled=True)  53.4 us
    dot_general x4, matrix products, rows_times_back(): lax.dot_general(left_rows, right_matrix, (((1,), (1,)), ((), ())), prefer...  51.6 us
    reduce_scatter x1, waiting for transfers between devices, local(): lax.psum_scatter(rows_times_back(pre_grad, up_weight).astype(jnp.bfloat16...  49.7 us
  transfers between devices with their start and end apart: 14, of which 12 were waited for; matrix products, arithmetic and copies ran while one was open for 25% of the time, Pallas kernels for 0%

commit v1 on v0

--- a/solution.py
+++ b/solution.py
@@ -1,12 +1,30 @@
+import functools
 import math
 import jax
 import jax.numpy as jnp
 from jax import lax
 from jax.sharding import PartitionSpec as P
+from jax.lax import axis_index, axis_size, ppermute
 
 HEAD_DIM = 128
 epsilon = 1e-05
 masked_score = -1e30
+
+
+def _lead_loops(patch, across):
+    n = axis_size(across)
+    heap = [(kk, (kk + 1) % n) for kk in range(n)]
+
+    def seats_all_apply(back):
+        if len(back) == n:
+            return back
+        return seats_all_apply([ppermute(back[0], axis_name=across, perm=heap), *back])
+
+    last = jnp.concatenate(seats_all_apply([patch]), axis=0)
+    return jnp.roll(last, shift=(axis_index(across) + 1) * patch.shape[0], axis=0)
+
+
+group_leaves = functools.partial(_lead_loops, across="mp")
 
 
 def norm_rows(values, gain):
@@ -134,7 +152,7 @@
         rows_times(hidden, down_weight).astype(jnp.bfloat16), "mp", scatter_dimension=0, tiled=True
     ).astype(jnp.float32)
     layer_output = (residual_mid + mlp_rows).astype(jnp.bfloat16)
-    cotangent_all = lax.all_gather(out_cotangent, "mp", axis=0, tiled=True)
+    cotangent_all = group_leaves(out_cotangent)
     down_weight_grad = jnp.einsum(
         "rf,rd->fd", hidden, cotangent_all, preferred_element_type=jnp.float32
     )

time: 1110 us -> 1160 us (1.045)
  waiting for transfers between devices: 616 us -> 648 us
  local copies, waits for them, and re-layouts: 78.1 us -> 95.3 us
    ppermute x0 -> x3, waiting for transfers between devices: none -> 153 us  [seats_all_apply(): ppermute(back[0], axis_name=across, perm=heap)]
    all_gather x1 -> x0, waiting for transfers between devices: 66.6 us -> none  [local(): cotangent_all = lax.all_gather(out_cotangent, 'mp', axis=0, tiled=True)]
    all_gather x1, waiting for transfers between devices: 53.4 us -> 0.01 us  [local(): lax.all_gather(normed_mlp.astype(jnp.bfloat16), 'mp', axis=0, tiled=True)]
    unnamed x56 -> x69, local copies, waits for them, and re-layouts: 3.2 us -> 19.3 us
  transfers between devices with their start and end apart: 14 -> 16, of which waited for: 12 -> 13; matrix products, arithmetic and copies ran while one was open for 25% -> 23% of each run, Pallas kernels for 0% -> 0%
where the time goes in v1:
time: 1160 us
  waiting for transfers between devices  648 us (56%)
  matrix products  284 us (24%)
  local copies, waits for them, and re-layouts  95.3 us (8%)
  other arithmetic  71.6 us (6%)
  blocking collectives  39.5 us (3%)
  between operations  14.5 us (1%)
    ppermute x3, waiting for transfers between devices, seats_all_apply(): ppermute(back[0], axis_name=across, perm=heap)  153 us
    all_gather x1, waiting for transfers between devices, local(): lax.all_gather(normed_attn.astype(jnp.bfloat16), 'mp', axis=0, tiled=True)  73 us
    reduce_scatter x1, waiting for transfers between devices, local(): lax.psum_scatter(rows_times(context_flat, out_weight).astype(jnp.bfloat16...  70.3 us
    reduce_scatter x1, waiting for transfers between devices, local(): lax.psum_scatter(attn_input_back(queries_grad, keys_grad, values_grad, qu...  70.1 us
    reduce_scatter x1, waiting for transfers between devices, local(): lax.psum_scatter(rows_times(hidden, down_weight).astype(jnp.bfloat16), 'm...  68.7 us
    dot_general x4, matrix products, rows_times_back(): lax.dot_general(left_rows, right_matrix, (((1,), (1,)), ((), ())), prefer...  51.7 us
    reduce_scatter x1, waiting for transfers between devices, local(): lax.psum_scatter(rows_times_back(pre_grad, up_weight).astype(jnp.bfloat16...  49.1 us
    psum x1, blocking collectives, local(): lax.psum((attn_gain_grad, mlp_gain_grad), ('dp', 'mp'))  39.5 us
  transfers between devices with their start and end apart: 16, of which 13 were waited for; matrix products, arithmetic and copies ran while one was open for 23% of the time, Pallas kernels for 0%

profile of v1, /device:TPU:0, one launch (start us, length us, event | category | flops | bytes accessed | tf_op | source)
XLA Modules:
  0.0 1158.7 jit_solution(5650380262211317874)
XLA Ops:
  14.0 73.0 %all-gather.4.cloned.1.call-done = bf16[1536,2048]{1,0:T(8,128)(2,1)} async-done(((bf16[384,2048]{1,0:T(8,128)(2,1)}), bf16[1536,2048]{1,0:T(8,128)(2,1)}) %all-gather.4.cloned.1.call-update) | async-done | bytes 6291472 | tf_op jit(solution)/shard_map/all_gather | solution.py:124
  127.7 28.2 %while.26 = (s32[]{:T(128)}, bf16[2,768,4,128]{3,2,1,0:T(4,128)(2,1)}, f32[2,4,768]{2,1,0:T(4,128)S(1)}, bf16[2,768,4,128]{3,2,1,0:T(4,128)(2,1)}, s32[2,768]{1,...) while((s32[]{:T(128)}, ...), condition=%wide.region_5.6_spmd, body=%wide.region_2.5_spmd.sunk | while | flops 1231352832 | bytes 43362440 | solution.py:137
  163.0 70.3 %reduce-scatter.11.cloned.1.call-done = bf16[384,2048]{1,0:T(8,128)(2,1)} async-done(((bf16[1536,2048]{1,0:T(8,128)(2,1)}), bf16[384,2048]{1,0:T(8,128)(2,1)}) %reduce-scatter.11.cloned.1.call-update) | async-done | bytes 1572880 | tf_op jit(solution)/shard_map/reduce_scatter | solution.py:139
  240.1 53.7 %collective-permute-done = bf16[384,2048]{1,0:T(8,128)(2,1)S(1)} collective-permute-done((bf16[384,2048]{1,0:T(8,128)(2,1)}, bf16[384,2048]{1,0:T(8,128)(2,1)S(1)}, u32[]{:S(2)}, u32[]{:S(2)}) %collective-permute-start) | collective-permute-done | bytes 1572896 | tf_op jit(solution)/shard_map/ppermute | solution.py:21
  297.0 63.4 %collective-permute-done.1 = bf16[384,2048]{1,0:T(8,128)(2,1)} collective-permute-done((bf16[384,2048]{1,0:T(8,128)(2,1)S(1)}, bf16[384,2048]{1,0:T(8,128)(2,1)}, u32[]{:S(2)}, u32[]{:S(2)}) %collective-permute-start.1) | collective-permute-done | bytes 1572896 | tf_op jit(solution)/shard_map/ppermute | solution.py:21
  360.8 36.2 %collective-permute-done.2 = bf16[384,2048]{1,0:T(8,128)(2,1)} collective-permute-done((bf16[384,2048]{1,0:T(8,128)(2,1)}, bf16[384,2048]{1,0:T(8,128)(2,1)}, u32[]{:S(2)}, u32[]{:S(2)}) %collective-permute-start.2) | collective-permute-done | bytes 1572896 | tf_op jit(solution)/shard_map/ppermute | solution.py:21
  413.2 18.9 %fusion.96 = f32[1536,2048]{1,0:T(8,128)} fusion(bf16[1536,2048]{1,0:T(8,128)(2,1)} %all-gather.6.cloned.1.call-done, bf16[2048,2048]{1,0:T(8,128)(2,1)} %param.21), kind=kOutput, calls=%fused_computation.159 | convolution fusion | flops 12884901888 | bytes 27262976 | tf_op jit(solution)/shard_map/dot_general | solution.py:148
  432.1 29.0 %fusion.48 = bf16[1536,2048]{1,0:T(8,128)(2,1)} fusion(f32[1536,2048]{1,0:T(8,128)} %fusion.96, bf16[2048,2048]{1,0:T(8,128)(2,1)} %param.22, bf16[3072,2048]{1,0:T(8,128)(2,1)} %constant_dynamic-update-slice_fusion.4, s32[]{:T(128)S(6)} %select_n.21), kind=kOutput, calls=%fused_computation.68 | convolution fusion | flops 12947816448 | bytes 33554436 | tf_op jit(solution)/shard_map/dot_general | solution.py:159
  461.1 19.1 %convolution_convert_fusion.4 = bf16[1536,2048]{1,0:T(8,128)(2,1)} fusion(bf16[1536,2048]{1,0:T(8,128)(2,1)} %fusion.48, bf16[2048,2048]{1,0:T(8,128)(2,1)} %param.21), kind=kOutput, calls=%fused_computation.73 | convolution fusion | flops 12888047616 | bytes 20971520 | tf_op jit(solution)/shard_map/dot_general | solution.py:51
  480.3 20.5 %convolution_convert_fusion.5 = bf16[1536,2048]{1,0:T(8,128)(2,1)} fusion(bf16[2048,2048]{1,0:T(8,128)(2,1)} %param.22, f32[1536,2048]{1,0:T(8,128)} %fusion.96), kind=kOutput, calls=%fused_computation.74 | convolution fusion | flops 12916359168 | bytes 27262976 | tf_op jit(solution)/shard_map/dot_general | solution.py:47
  500.9 49.1 %reduce-scatter.15.cloned.1.call-done = bf16[384,2048]{1,0:T(8,128)(2,1)} async-done(((bf16[1536,2048]{1,0:T(8,128)(2,1)}), bf16[384,2048]{1,0:T(8,128)(2,1)}) %reduce-scatter.15.cloned.1.call-update) | async-done | bytes 1572880 | tf_op jit(solution)/shard_map/reduce_scatter | solution.py:166
  554.4 68.7 %reduce-scatter.13.cloned.1.call-done = bf16[384,2048]{1,0:T(8,128)(2,1)} async-done(((bf16[1536,2048]{1,0:T(8,128)(2,1)}), bf16[384,2048]{1,0:T(8,128)(2,1)}) %reduce-scatter.13.cloned.1.call-update) | async-done | bytes 1572880 | tf_op jit(solution)/shard_map/reduce_scatter | solution.py:151
  632.0 23.9 %convolution_convert_fusion.2 = bf16[2048,2048]{1,0:T(8,128)(2,1)} fusion(bf16[3072,2048]{1,0:T(8,128)(2,1)} %constant_dynamic-update-slice_fusion.4, s32[]{:T(128)S(6)} %select_n.21, f32[1536,2048]{1,0:T(8,128)} %fusion.96), kind=kOutput, calls=%fused_computation.71 | convolution fusion | flops 12917407744 | bytes 27262980 | tf_op jit(solution)/shard_map/rf,rd->fd/dot_general | solution.py:156
  655.9 19.7 %convolution_convert_fusion.3 = bf16[2048,2048]{1,0:T(8,128)(2,1)} fusion(bf16[1536,2048]{1,0:T(8,128)(2,1)} %all-gather.6.cloned.1.call-done, bf16[1536,2048]{1,0:T(8,128)(2,1)} %fusion.48), kind=kOutput, calls=%fused_computation.72 | convolution fusion | flops 12889096192 | bytes 20971520 | tf_op jit(solution)/shard_map/rd,rf->df/dot_general | solution.py:163
  675.7 26.5 %all-gather.8.cloned.1.call-done = bf16[1536,2048]{1,0:T(8,128)(2,1)} async-done(((bf16[384,2048]{1,0:T(8,128)(2,1)}), bf16[1536,2048]{1,0:T(8,128)(2,1)}) %all-gather.8.cloned.1.call-update) | async-done | bytes 6291472 | tf_op jit(solution)/shard_map/all_gather | solution.py:174
  726.1 99.5 %while.27 = (s32[]{:T(128)}, bf16[2,768,4,128]{3,2,1,0:T(4,128)(2,1)}, bf16[2,768,4,128]{3,2,1,0:T(4,128)(2,1)}, bf16[2,768,4,128]{3,2,1,0:T(4,128)(2,1)}, bf16[...) while((s32[]{:T(128)}, ...), condition=%wide.region_15.16_spmd, body=%wide.region_13.15_spmd.sunk | while | flops 3051156480 | bytes 169179440 | solution.py:181
  798.6 11.5 multiply_convert_fusion.7
  867.0 15.8 %add_convert_fusion = bf16[1536,2048]{1,0:T(8,128)(2,1)} fusion(f32[1536,2048]{1,0:T(8,128)} %fusion.74, f32[1536,2048]{1,0:T(8,128)} %fusion.77, bf16[2048,512]{1,0:T(8,128)(2,1)} %param.17, bf16[192,8,4,128]{3,2,1,0:T(4,128)(2,1)} %bitcast.145), kind=kOutput, calls=%fused_computation.69 | convolution fusion | flops 3233808384 | bytes 35127296 | tf_op jit(solution)/shard_map/dot_general | solution.py:51
  888.4 32.5 %reduce-scatter.25.cloned.1.call-done = bf16[512,256]{1,0:T(8,128)(2,1)} async-done(((bf16[512,2048]{1,0:T(8,128)(2,1)}), bf16[512,256]{1,0:T(8,128)(2,1)}) %reduce-scatter.25.cloned.1.call-update) | async-done | bytes 262160 | tf_op jit(solution)/shard_map/reduce_scatter | solution.py:232
  922.7 34.7 %reduce-scatter.19.cloned.1.call-done = bf16[256,512]{1,0:T(8,128)(2,1)} async-done(((bf16[2048,512]{1,0:T(8,128)(2,1)}), bf16[256,512]{1,0:T(8,128)(2,1)}) %reduce-scatter.19.cloned.1.call-update) | async-done | bytes 262160 | tf_op jit(solution)/shard_map/reduce_scatter | solution.py:223
  959.2 35.0 %reduce-scatter.23.cloned.1.call-done = bf16[256,512]{1,0:T(8,128)(2,1)} async-done(((bf16[2048,512]{1,0:T(8,128)(2,1)}), bf16[256,512]{1,0:T(8,128)(2,1)}) %reduce-scatter.23.cloned.1.call-update) | async-done | bytes 262160 | tf_op jit(solution)/shard_map/reduce_scatter | solution.py:229
  996.0 34.8 %reduce-scatter.21.cloned.1.call-done = bf16[256,512]{1,0:T(8,128)(2,1)} async-done(((bf16[2048,512]{1,0:T(8,128)(2,1)}), bf16[256,512]{1,0:T(8,128)(2,1)}) %reduce-scatter.21.cloned.1.call-update) | async-done | bytes 262160 | tf_op jit(solution)/shard_map/reduce_scatter | solution.py:226
  1032.6 70.1 %reduce-scatter.17.cloned.1.call-done = bf16[384,2048]{1,0:T(8,128)(2,1)} async-done(((bf16[1536,2048]{1,0:T(8,128)(2,1)}), bf16[384,2048]{1,0:T(8,128)(2,1)}) %reduce-scatter.17.cloned.1.call-update) | async-done | bytes 1572880 | tf_op jit(solution)/shard_map/reduce_scatter | solution.py:198
  1107.1 39.5 %all-reduce = (f32[2048]{0:T(1024)}, f32[2048]{0:T(1024)}) all-reduce(f32[2048]{0:T(1024)S(1)} %get-tuple-element.143, f32[2048]{0:T(1024)S(1)} %copy-done.30), channel_id=1, replica_groups=mesh['dp'=8,'mp'=4] {'dp','mp'}, use_global_device_ids=true, to_apply=%region_26.27 | all-reduce | flops 4096 | bytes 32768 | tf_op jit(solution)/shard_map/psum | solution.py:214
  (225 shorter events, 297.7 us)
Async XLA Ops:
  7.2 148.7 %copy-start = (bf16[512,2048]{1,0:T(8,128)(2,1)S(1)}, bf16[512,2048]{1,0:T(8,128)(2,1)}, u32[]{:S(2)}) copy-start(bf16[512,2048]{1,0:T(8,128)(2,1)} %param.20) | copy-start | bytes 6291460
  7.2 79.8 %all-gather.4.cloned.1.call-start = ((), (), s32[]{:S(2)}) async-start(), calls=%async_computation.10 | async-start | bytes 7864320 | tf_op jit(solution)/shard_map/all_gather | solution.py:124
  14.0 219.3 %reduce-scatter.11.cloned.1.call-start = ((), (), s32[]{:S(2)}) async-start(), calls=%async_computation.11 | async-start | bytes 7864320 | tf_op jit(solution)/shard_map/reduce_scatter | solution.py:139
  162.9 73.9 %copy-start.27 = (f32[2048]{0:T(1024)S(1)}, f32[2048]{0:T(1024)}, u32[]{:S(2)}) copy-start(f32[2048]{0:T(1024)} %param.24) | copy-start | bytes 24580
  162.9 250.3 %all-gather.6.cloned.1.call-start = ((), (), s32[]{:S(2)}) async-start(), calls=%async_computation.12 | async-start | bytes 7864320 | tf_op jit(solution)/shard_map/all_gather | solution.py:147
  238.7 311.4 %reduce-scatter.15.cloned.1.call-start = ((), (), s32[]{:S(2)}) async-start(), calls=%async_computation.14 | async-start | bytes 7864320 | tf_op jit(solution)/shard_map/reduce_scatter | solution.py:166
  238.7 55.0 %collective-permute-start = (bf16[384,2048]{1,0:T(8,128)(2,1)}, bf16[384,2048]{1,0:T(8,128)(2,1)S(1)}, u32[]{:S(2)}, u32[]{:S(2)}) collective-permute-start(bf16[384,2048]{1,0:T(8,128)(2,1)} %param.25), channel_id=1, source_target_pairs={{0,1},{1,2},{2,3},{3,0},{4,5},{5,6},{6,7},{7,4},{8,9},{9,10},{10,1... | collective-permute-start | bytes 4718600 | tf_op jit(solution)/shard_map/ppermute | solution.py:21
  294.9 65.5 %collective-permute-start.1 = (bf16[384,2048]{1,0:T(8,128)(2,1)S(1)}, bf16[384,2048]{1,0:T(8,128)(2,1)}, u32[]{:S(2)}, u32[]{:S(2)}) collective-permute-start(bf16[384,2048]{1,0:T(8,128)(2,1)S(1)} %collective-permute-done), channel_id=1, source_target_pairs={{0,1},{1,2},{2,3},{3,0},{4,5},{5,6},{6,7},{7,4},{8,9},{9,10},{10,1... | collective-permute-start | bytes 4718600 | tf_op jit(solution)/shard_map/ppermute | solution.py:21
  360.4 36.7 %collective-permute-start.2 = (bf16[384,2048]{1,0:T(8,128)(2,1)}, bf16[384,2048]{1,0:T(8,128)(2,1)}, u32[]{:S(2)}, u32[]{:S(2)}) collective-permute-start(bf16[384,2048]{1,0:T(8,128)(2,1)} %collective-permute-done.1), channel_id=1, source_target_pairs={{0,1},{1,2},{2,3},{3,0},{4,5},{5,6},{6,7},{7,4},{8,9},{9,10},{10,1... | collective-permute-start | bytes 4718600 | tf_op jit(solution)/shard_map/ppermute | solution.py:21
  480.3 142.8 %reduce-scatter.13.cloned.1.call-start = ((), (), s32[]{:S(2)}) async-start(), calls=%async_computation.13 | async-start | bytes 7864320 | tf_op jit(solution)/shard_map/reduce_scatter | solution.py:151
  500.9 201.3 %all-gather.8.cloned.1.call-start = ((), (), s32[]{:S(2)}) async-start(), calls=%async_computation.15 | async-start | bytes 7864320 | tf_op jit(solution)/shard_map/all_gather | solution.py:174
  631.9 251.0 %reduce-scatter.29.cloned.1.call-start = ((), (), s32[]{:S(2)}) async-start(), calls=%async_computation.22 | async-start | bytes 9437184 | tf_op jit(solution)/shard_map/reduce_scatter | solution.py:238
  655.9 229.7 %reduce-scatter.27.cloned.1.call-start = ((), (), s32[]{:S(2)}) async-start(), calls=%async_computation.21 | async-start | bytes 9437184 | tf_op jit(solution)/shard_map/reduce_scatter | solution.py:235
  675.7 245.2 %reduce-scatter.25.cloned.1.call-start = ((), (), s32[]{:S(2)}) async-start(), calls=%async_computation.20 | async-start | bytes 2359296 | tf_op jit(solution)/shard_map/reduce_scatter | solution.py:232
  721.3 236.0 %reduce-scatter.19.cloned.1.call-start = ((), (), s32[]{:S(2)}) async-start(), calls=%async_computation.17 | async-start | bytes 2359296 | tf_op jit(solution)/shard_map/reduce_scatter | solution.py:223
  833.6 160.5 %reduce-scatter.23.cloned.1.call-start = ((), (), s32[]{:S(2)}) async-start(), calls=%async_computation.19 | async-start | bytes 2359296 | tf_op jit(solution)/shard_map/reduce_scatter | solution.py:229
  841.7 189.0 %reduce-scatter.21.cloned.1.call-start = ((), (), s32[]{:S(2)}) async-start(), calls=%async_computation.18 | async-start | bytes 2359296 | tf_op jit(solution)/shard_map/reduce_scatter | solution.py:226
  849.9 252.7 %reduce-scatter.17.cloned.1.call-start = ((), (), s32[]{:S(2)}) async-start(), calls=%async_computation.16 | async-start | bytes 7864320 | tf_op jit(solution)/shard_map/reduce_scatter | solution.py:198
  885.6 217.0 %copy-start.24 = (f32[2048]{0:T(1024)S(1)}, f32[2048]{0:T(1024)}, u32[]{:S(2)}) copy-start(f32[2048]{0:T(1024)} %param.23) | copy-start | bytes 24580
  885.6 217.0 %copy-start.26 = (f32[384]{0:T(512)S(1)}, f32[384]{0:T(512)}, u32[]{:S(2)}) copy-start(f32[384]{0:T(512)} %copy-done.25) | copy-start | bytes 4612
  888.4 217.0 %copy-start.34 = (f32[384]{0:T(512)S(1)}, f32[384]{0:T(512)}, u32[]{:S(2)}) copy-start(f32[384]{0:T(512)} %copy-done.33) | copy-start | bytes 4612
  888.4 217.1 %copy-start.29 = (f32[384]{0:T(512)S(1)}, f32[384]{0:T(512)}, u32[]{:S(2)}) copy-start(f32[384]{0:T(512)} %copy-done.28) | copy-start | bytes 4612
  1032.5 74.5 %copy-start.30 = (f32[2048]{0:T(1024)S(1)}, f32[2048]{0:T(1024)}, u32[]{:S(2)}) copy-start(f32[2048]{0:T(1024)} %get-tuple-element.141) | copy-start | bytes 24580
  1032.5 114.0 %copy-start.32 = (f32[384]{0:T(512)S(1)}, f32[384]{0:T(512)}, u32[]{:S(2)}) copy-start(f32[384]{0:T(512)} %copy-done.31) | copy-start | bytes 4612
  (35 other events, 176.8 us)
Sparse Core Ops, SparseCore 0:
  14.1 72.8 all-gather.3
  163.0 70.1 reduce-scatter.10
  238.8 117.2 all-gather.5
  480.4 69.6 reduce-scatter.14
  552.9 70.1 reduce-scatter.12
  632.0 70.1 all-gather.7
  704.5 89.5 reduce-scatter.28
  796.4 87.9 reduce-scatter.26
  886.7 34.0 reduce-scatter.24
  923.0 34.3 reduce-scatter.18
  959.7 34.4 reduce-scatter.22
  996.3 34.3 reduce-scatter.20
  1033.7 68.8 reduce-scatter.16
